TPU v7x, 32 devices: a whole 2x2x4 slice. The times are simulated.
32 devices in a mesh: stream: 4 (over y, x), ctx: 4 (over z), head: 2 (over core).
Axes of the slice: x: 2, y: 2, z: 4, core: 2. Of those that a mesh axis runs over, the one named last changes fastest.
Arguments:
- tokens: bfloat16 [4, 1024, 2048], P('stream', 'ctx'), may hold values from -6 to 6
- doc_lengths: int32 [4, 6], P('stream'), may hold values from 1 to 512, 1024 in all within a row
- ln1_gain: bfloat16 [2048], replicated, may hold values from 0.25 to 1.75
- ln1_bias: bfloat16 [2048], replicated, may hold values from -1.5 to 1.5
- qkv_weight: bfloat16 [3, 2048, 2048], P(None, 'ctx', 'head'), may hold values from -0.125 to 0.125
- qkv_bias: bfloat16 [3, 2048], P(None, 'head'), may hold values from -0.5 to 0.5
- out_weight: bfloat16 [2048, 2048], P('head', 'ctx'), may hold values from -1 to 1
- out_bias: bfloat16 [2048], replicated, may hold values from -3 to 3
- ln2_gain: bfloat16 [2048], replicated, may hold values from 0.25 to 1.75
- ln2_bias: bfloat16 [2048], replicated, may hold values from -1.5 to 1.5
- up_weight: bfloat16 [2048, 8192], P('ctx', 'head'), may hold values from -0.125 to 0.125
- up_bias: bfloat16 [8192], P('head'), may hold values from -1.5 to 1.5
- down_weight: bfloat16 [8192, 2048], P('head', 'ctx'), may hold values from -0.0625 to 0.0625
- down_bias: bfloat16 [2048], replicated, may hold values from -3 to 3
- cotangent: bfloat16 [4, 1024, 2048], P('stream', 'ctx'), may hold values from -6 to 6
Outputs:
- output: bfloat16 [4, 1024, 2048], P('stream', 'ctx')
- input_grad: float32 [4, 1024, 2048], P('stream', 'ctx')
- ln1_gain_grad: float32 [2048], replicated
- ln1_bias_grad: float32 [2048], replicated
- qkv_weight_grad: float32 [3, 2048, 2048], P(None, 'ctx', 'head')
- qkv_bias_grad: float32 [3, 2048], P(None, 'head')
- out_weight_grad: float32 [2048, 2048], P('head', 'ctx')
- out_bias_grad: float32 [2048], replicated
- ln2_gain_grad: float32 [2048], replicated
- ln2_bias_grad: float32 [2048], replicated
- up_weight_grad: float32 [2048, 8192], P('ctx', 'head')
- up_bias_grad: float32 [8192], P('head')
- down_weight_grad: float32 [8192, 2048], P('head', 'ctx')
- down_bias_grad: float32 [2048], replicated
Inputs may be any that keep to these rules, and one draw needn't show every extreme that they name: `doc_lengths`: each sequence's 6 document lengths sum to 1024, the documents lie end to end in the given order, and the longest has exactly 512 tokens.
All inputs are finite; a program needn't handle non-finite values.
Results may differ from a plain program's by a relative error of at most 0.025.
Values may be sent and summed in bfloat16 or wider, within the bound.
A program may use at most 256 MiB of HBM per device.

v0:
```python
from functools import partial
import math
import jax
import jax.numpy as jnp
from jax import lax
from jax.sharding import PartitionSpec as P

HEAD = 256
ROT = 64


def layer_norm(values, gain, offset):
    centre = jnp.mean(values, axis=-1, keepdims=True)
    centred = values - centre
    spread = jnp.mean(centred * centred, axis=-1, keepdims=True)
    return centred * lax.rsqrt(spread + 1e-05) * gain + offset


def rotary(values, angles):
    half = angles.shape[-1]
    cosine = jnp.cos(angles)[:, None, :]
    sine = jnp.sin(angles)[:, None, :]
    first = values[..., :half]
    second = values[..., half : 2 * half]
    return jnp.concatenate(
        [first * cosine - second * sine, second * cosine + first * sine, values[..., 2 * half :]],
        axis=-1,
    )


def doc_starts(doc_sizes, positions):
    ends = jnp.cumsum(doc_sizes)
    starts = ends - doc_sizes
    return jnp.max(jnp.where(starts[None, :] <= positions[:, None], starts[None, :], 0), axis=1)


def per_device(
    tokens,
    doc_lengths,
    ln1_gain,
    ln1_bias,
    qkv_weight,
    qkv_bias,
    out_weight,
    out_bias,
    ln2_gain,
    ln2_bias,
    up_weight,
    up_bias,
    down_weight,
    down_bias,
    cotangent,
):
    inputs = tokens[0].astype(jnp.float32)
    count = inputs.shape[0]
    ctx_count = lax.axis_size("ctx")
    length = count * ctx_count
    positions = lax.axis_index("ctx") * count + jnp.arange(count, dtype=jnp.int32)
    starts = doc_starts(doc_lengths[0], positions)
    frequency = 10000.0 ** (-jnp.arange(0, ROT, 2, dtype=jnp.float32) / ROT)
    angles = (positions - starts).astype(jnp.float32)[:, None] * frequency[None, :]
    scale = HEAD ** (-0.5)
    full_qkv, full_out, full_up, full_down = (
        lax.all_gather(qkv_weight, "ctx", axis=1, tiled=True),
        lax.all_gather(out_weight, "ctx", axis=1, tiled=True),
        lax.all_gather(up_weight, "ctx", axis=0, tiled=True),
        lax.all_gather(down_weight, "ctx", axis=1, tiled=True),
    )
    gain_one = ln1_gain.astype(jnp.float32)
    offset_one = ln1_bias.astype(jnp.float32)
    gain_two = ln2_gain.astype(jnp.float32)
    offset_two = ln2_bias.astype(jnp.float32)
    low_one = layer_norm(inputs, gain_one, offset_one).astype(jnp.bfloat16)
    low_two = layer_norm(inputs, gain_two, offset_two).astype(jnp.bfloat16)
    projected = (
        jnp.einsum("nd,cde->cne", low_one, full_qkv, preferred_element_type=jnp.float32)
        + qkv_bias.astype(jnp.float32)[:, None, :]
    )
    width = projected.shape[2]
    local_heads = width // HEAD
    query = rotary(projected[0].reshape(count, local_heads, HEAD), angles).astype(jnp.bfloat16)
    keys_flat = (
        rotary(projected[1].reshape(count, local_heads, HEAD), angles)
        .reshape(count, width)
        .astype(jnp.bfloat16)
    )
    values_flat = projected[2].astype(jnp.bfloat16)
    all_keys, all_values = (
        lax.all_gather(keys_flat, "ctx", axis=0, tiled=True),
        lax.all_gather(values_flat, "ctx", axis=0, tiled=True),
    )
    block = math.gcd(length, 512)
    block_count = length // block
    key_blocks = all_keys.reshape(block_count, block, local_heads, HEAD)
    value_blocks = all_values.reshape(block_count, block, local_heads, HEAD)
    firsts = jnp.arange(block_count, dtype=jnp.int32) * block

    def block_scores(key_block, first):
        key_index = first + jnp.arange(block, dtype=jnp.int32)
        allowed = (key_index[None, :] <= positions[:, None]) & (
            key_index[None, :] >= starts[:, None]
        )
        scores = (
            jnp.einsum("qhe,khe->hqk", query, key_block, preferred_element_type=jnp.float32) * scale
        )
        return (jnp.where(allowed[None], scores, -1e30), allowed[None])

    def statistics(carry, item):
        running, norm_sum = carry
        key_block, first = item
        masked, allowed = block_scores(key_block, first)
        newest = jnp.maximum(running, jnp.max(masked, axis=-1))
        raised = jnp.where(allowed, jnp.exp(masked - newest[..., None]), 0.0)
        norm_sum = norm_sum * jnp.exp(running - newest) + jnp.sum(raised, axis=-1)
        return ((newest, norm_sum), None)

    initial = (
        jnp.full((local_heads, count), -1e30, jnp.float32),
        jnp.zeros((local_heads, count), jnp.float32),
    )
    (running, norm_sum), _ = lax.scan(statistics, initial, (key_blocks, firsts))
    log_norm = running + jnp.log(norm_sum)

    def share_block(key_block, first):
        masked, allowed = block_scores(key_block, first)
        return jnp.where(allowed, jnp.exp(masked - log_norm[..., None]), 0.0)

    def accumulate(mixed, item):
        key_block, value_block, first = item
        shares_low = share_block(key_block, first).astype(jnp.bfloat16)
        return (
            mixed
            + jnp.einsum(
                "hqk,khe->qhe", shares_low, value_block, preferred_element_type=jnp.float32
            ),
            None,
        )

    mixed, _ = lax.scan(
        accumulate,
        jnp.zeros((count, local_heads, HEAD), jnp.float32),
        (key_blocks, value_blocks, firsts),
    )
    mixed_low = mixed.reshape(count, width).astype(jnp.bfloat16)
    attention = jnp.dot(mixed_low, full_out, preferred_element_type=jnp.float32)
    hidden = jnp.dot(low_two, full_up, preferred_element_type=jnp.float32) + up_bias.astype(
        jnp.float32
    )
    activated = jax.nn.gelu(hidden, approximate=False).astype(jnp.bfloat16)
    branches = attention + jnp.dot(activated, full_down, preferred_element_type=jnp.float32)
    joint = lax.psum(branches.astype(jnp.bfloat16), "head").astype(jnp.float32)
    output = inputs + joint + out_bias.astype(jnp.float32) + down_bias.astype(jnp.float32)
    upstream = cotangent[0]
    down_grad = jnp.dot(activated.T, upstream, preferred_element_type=jnp.float32)
    activated_grad = jnp.dot(upstream, full_down.T, preferred_element_type=jnp.float32)
    _, gelu_back = jax.vjp(partial(jax.nn.gelu, approximate=False), hidden)
    hidden_grad = gelu_back(activated_grad)[0].astype(jnp.bfloat16)
    up_grad = jnp.dot(low_two.T, hidden_grad, preferred_element_type=jnp.float32)
    up_bias_grad = jnp.sum(hidden_grad.astype(jnp.float32), axis=0)
    normed_two_grad = jnp.dot(hidden_grad, full_up.T, preferred_element_type=jnp.float32)
    out_grad = jnp.dot(mixed_low.T, upstream, preferred_element_type=jnp.float32)
    mixed_grad = jnp.dot(upstream, full_out.T, preferred_element_type=jnp.float32).astype(
        jnp.bfloat16
    )
    mixed_grad_heads = mixed_grad.reshape(count, local_heads, HEAD)
    delta = jnp.sum(mixed_grad_heads.astype(jnp.float32) * mixed, axis=-1).T

    def backward_block(query_grad, item):
        key_block, value_block, first = item
        shares = share_block(key_block, first)
        share_grad = jnp.einsum(
            "qhe,khe->hqk", mixed_grad_heads, value_block, preferred_element_type=jnp.float32
        )
        score_grad = (shares * (share_grad - delta[..., None])).astype(jnp.bfloat16)
        query_grad = (
            query_grad
            + jnp.einsum("hqk,khe->qhe", score_grad, key_block, preferred_element_type=jnp.float32)
            * scale
        )
        key_grad = (
            jnp.einsum("hqk,qhe->khe", score_grad, query, preferred_element_type=jnp.float32)
            * scale
        )
        value_grad = jnp.einsum(
            "hqk,qhe->khe",
            shares.astype(jnp.bfloat16),
            mixed_grad_heads,
            preferred_element_type=jnp.float32,
        )
        return (
            query_grad,
            jnp.concatenate(
                [key_grad.reshape(block, width), value_grad.reshape(block, width)], axis=1
            ),
        )

    query_grad, key_terms = lax.scan(
        backward_block,
        jnp.zeros((count, local_heads, HEAD), jnp.float32),
        (key_blocks, value_blocks, firsts),
    )
    own_grads = lax.psum_scatter(
        key_terms.reshape(length, 2 * width).astype(jnp.bfloat16),
        "ctx",
        scatter_dimension=0,
        tiled=True,
    ).astype(jnp.float32)
    query_pre = rotary(query_grad, -angles).reshape(count, width)
    key_pre = rotary(own_grads[:, :width].reshape(count, local_heads, HEAD), -angles).reshape(
        count, width
    )
    projected_grad = jnp.stack([query_pre, key_pre, own_grads[:, width:]]).astype(jnp.bfloat16)
    qkv_grad = jnp.einsum(
        "nd,cne->cde", low_one, projected_grad, preferred_element_type=jnp.float32
    )
    qkv_bias_grad = jnp.sum(projected_grad.astype(jnp.float32), axis=1)
    normed_one_grad = jnp.einsum(
        "cne,cde->nd", projected_grad, full_qkv, preferred_element_type=jnp.float32
    )
    normed_one_grad, normed_two_grad = (
        lax.psum(normed_one_grad.astype(jnp.bfloat16), "head").astype(jnp.float32),
        lax.psum(normed_two_grad.astype(jnp.bfloat16), "head").astype(jnp.float32),
    )
    _, norm_back_one = jax.vjp(layer_norm, inputs, gain_one, offset_one)
    input_one, gain_grad_one, offset_grad_one = norm_back_one(normed_one_grad)
    _, norm_back_two = jax.vjp(layer_norm, inputs, gain_two, offset_two)
    input_two, gain_grad_two, offset_grad_two = norm_back_two(normed_two_grad)
    upstream_wide = upstream.astype(jnp.float32)
    input_grad = upstream_wide + input_one + input_two
    bias_grad = jnp.sum(upstream_wide, axis=0)
    small = lax.psum(
        (
            gain_grad_one,
            offset_grad_one,
            qkv_bias_grad,
            bias_grad,
            gain_grad_two,
            offset_grad_two,
            up_bias_grad,
        ),
        ("stream", "ctx"),
    )
    slices = (
        lax.psum_scatter(
            qkv_grad.astype(jnp.bfloat16), "ctx", scatter_dimension=1, tiled=True
        ).astype(jnp.float32),
        lax.psum_scatter(
            out_grad.astype(jnp.bfloat16), "ctx", scatter_dimension=1, tiled=True
        ).astype(jnp.float32),
        lax.psum_scatter(
            up_grad.astype(jnp.bfloat16), "ctx", scatter_dimension=0, tiled=True
        ).astype(jnp.float32),
        lax.psum_scatter(
            down_grad.astype(jnp.bfloat16), "ctx", scatter_dimension=1, tiled=True
        ).astype(jnp.float32),
    )
    shards = (
        lax.psum(slices[0].astype(jnp.bfloat16), "stream").astype(jnp.float32),
        lax.psum(slices[1].astype(jnp.bfloat16), "stream").astype(jnp.float32),
        lax.psum(slices[2].astype(jnp.bfloat16), "stream").astype(jnp.float32),
        lax.psum(slices[3].astype(jnp.bfloat16), "stream").astype(jnp.float32),
    )
    return (
        output.astype(jnp.bfloat16)[None],
        input_grad[None],
        small[0],
        small[1],
        shards[0],
        small[2],
        shards[1],
        small[3],
        small[4],
        small[5],
        shards[2],
        small[6],
        shards[3],
        small[3],
    )


def solution(mesh):
    in_specs = (
        P("stream", "ctx", None),
        P("stream", None),
        P(),
        P(),
        P(None, "ctx", "head"),
        P(None, "head"),
        P("head", "ctx"),
        P(),
        P(),
        P(),
        P("ctx", "head"),
        P("head"),
        P("head", "ctx"),
        P(),
        P("stream", "ctx", None),
    )
    out_specs = (
        P("stream", "ctx", None),
        P("stream", "ctx", None),
        P(),
        P(),
        P(None, "ctx", "head"),
        P(None, "head"),
        P("head", "ctx"),
        P(),
        P(),
        P(),
        P("ctx", "head"),
        P("head"),
        P("head", "ctx"),
        P(),
    )
    return jax.shard_map(
        per_device, mesh=mesh, in_specs=in_specs, out_specs=out_specs, check_vma=False
    )
```

profile of v0, /device:TPU:0, one launch (start us, length us, event | category | flops | bytes accessed | tf_op | source)
XLA Modules:
  0.0 2362.3 jit_solution(6158996267998633471)
XLA Ops:
  10.8 219.8 %all-gather.8.cloned.1.call-done = bf16[3,2048,1024]{2,1,0:T(8,128)(2,1)} async-done(((bf16[3,512,1024]{2,1,0:T(8,128)(2,1)}), bf16[3,2048,1024]{2,1,0:T(8,128)(2,1)}) %all-gather.8.cloned.1.call-update) | async-done | bytes 12582928 | tf_op jit(solution)/shard_map/all_gather | solution.py:64
  249.2 61.9 %all-gather.12.cloned.1.call-done = bf16[1024,2048]{1,0:T(8,128)(2,1)} async-done(((bf16[1024,512]{1,0:T(8,128)(2,1)}), bf16[1024,2048]{1,0:T(8,128)(2,1)}) %all-gather.12.cloned.1.call-update) | async-done | bytes 4194320 | tf_op jit(solution)/shard_map/all_gather | solution.py:65
  315.9 41.9 %all-gather.10.cloned.1.call-done = bf16[1024,1024]{1,0:T(8,128)(2,1)} async-done(((bf16[256,1024]{1,0:T(8,128)(2,1)}), bf16[1024,1024]{1,0:T(8,128)(2,1)}) %all-gather.10.cloned.1.call-update) | async-done | bytes 2097168 | tf_op jit(solution)/shard_map/all_gather | solution.py:89
  362.7 41.8 %all-gather.18.cloned.1.call-done = bf16[1,1024,1024]{2,1,0:T(8,128)(2,1)} async-done(((bf16[1,256,1024]{2,1,0:T(8,128)(2,1)}), bf16[1,1024,1024]{2,1,0:T(8,128)(2,1)}) %all-gather.18.cloned.1.call-update) | async-done | bytes 2097168 | tf_op jit(solution)/shard_map/all_gather | solution.py:90
  409.0 7.8 while.37
  416.8 14.8 while.38
  434.3 29.0 %while.39 = (s32[]{:T(128)}, f32[256,4,256]{0,2,1:T(8,128)}, bf16[2,512,2048]{1,2,0:T(8,128)(2,1)}, bf16[2,512,4,256]{3,1,2,0:T(8,128)(2,1)}, s32[2]{0:T(128)S(1...) while((s32[]{:T(128)}, f32[256,4,256]{0,2,1:T(8,128)}, ...), condition=%wide.region_13.14_spmd.clone, body=%wide.region_12.13_spmd.clone.sunk | while | flops 1352794880 | bytes 31735028 | solution.py:197
  471.3 220.1 %all-gather.14.cloned.1.call-done = bf16[2048,4096]{1,0:T(8,128)(2,1)} async-done(((bf16[512,4096]{1,0:T(8,128)(2,1)}), bf16[2048,4096]{1,0:T(8,128)(2,1)}) %all-gather.14.cloned.1.call-update) | async-done | bytes 16777232 | tf_op jit(solution)/shard_map/all_gather | solution.py:66
  691.4 18.6 multiply_convert_fusion
  710.0 267.8 %all-gather.16.cloned.1.call-done = bf16[4096,2048]{1,0:T(8,128)(2,1)} async-done(((bf16[4096,512]{1,0:T(8,128)(2,1)}), bf16[4096,2048]{1,0:T(8,128)(2,1)}) %all-gather.16.cloned.1.call-update) | async-done | bytes 16777232 | tf_op jit(solution)/shard_map/all_gather | solution.py:67
  977.8 8.9 fusion.102
  989.6 19.1 convert_reduce_fusion
  1008.7 12.0 convolution_convert_fusion.3
  1020.7 35.0 %reduce-scatter.6.cloned.1.call-done = bf16[256,2048]{1,0:T(8,128)(2,1)} async-done(((bf16[1024,2048]{1,0:T(8,128)(2,1)}), bf16[256,2048]{1,0:T(8,128)(2,1)}) %reduce-scatter.6.cloned.1.call-update) | async-done | bytes 1048592 | tf_op jit(solution)/shard_map/reduce_scatter | solution.py:202
  1074.4 9.3 fusion.64
  1088.2 8.0 convert_bitcast_fusion
  1096.2 11.0 convolution_convert_fusion.1
  1107.3 9.8 convolution_convert_fusion
  1131.7 56.9 %reduce-scatter.10.cloned.1.call-done = bf16[1024,512]{1,0:T(8,128)(2,1)} async-done(((bf16[1024,2048]{1,0:T(8,128)(2,1)}), bf16[1024,512]{1,0:T(8,128)(2,1)}) %reduce-scatter.10.cloned.1.call-update) | async-done | bytes 1048592 | tf_op jit(solution)/shard_map/reduce_scatter | solution.py:247
  1188.6 214.7 %reduce-scatter.8.cloned.1.call-done = bf16[3,512,1024]{1,2,0:T(8,128)(2,1)} async-done(((bf16[3,2048,1024]{1,2,0:T(8,128)(2,1)}), bf16[3,512,1024]{1,2,0:T(8,128)(2,1)}) %reduce-scatter.8.cloned.1.call-update) | async-done | bytes 3145744 | tf_op jit(solution)/shard_map/reduce_scatter | solution.py:244
  1403.3 283.9 %reduce-scatter.12.cloned.1.call-done = bf16[512,4096]{1,0:T(8,128)(2,1)} async-done(((bf16[2048,4096]{1,0:T(8,128)(2,1)}), bf16[512,4096]{1,0:T(8,128)(2,1)}) %reduce-scatter.12.cloned.1.call-update) | async-done | bytes 4194320 | tf_op jit(solution)/shard_map/reduce_scatter | solution.py:250
  1687.2 283.3 %reduce-scatter.14.cloned.1.call-done = bf16[4096,512]{1,0:T(8,128)(2,1)} async-done(((bf16[4096,2048]{1,0:T(8,128)(2,1)}), bf16[4096,512]{1,0:T(8,128)(2,1)}) %reduce-scatter.14.cloned.1.call-update) | async-done | bytes 4194320 | tf_op jit(solution)/shard_map/reduce_scatter | solution.py:253
  1970.5 116.1 %all-reduce.7.cloned.1.call-done = (f32[2048]{0:T(1024)}, f32[2048]{0:T(1024)}, f32[3,1024]{1,0:T(4,128)}, f32[2048]{0:T(1024)}, f32[2048]{0:T(1024)}, /*index=5*/f32[2048]{0:T(1024)}, f32[4096]{0:T(1024)}) async-done(((f32[2048]{0:T(1024)}, f32[2048]{0:T(1024)}, f32[3,1024]{1,0:T(4,128)}, f32[2048]{0:T(1024)}, f32[2048]{0:T(1024)}, /*index=5*/f32[2048]{0:T(1024)}, f32[4096]{0:T(1024)}), (f32[2048]{0:T(1024)}, ...) | async-done | bytes 69648 | tf_op jit(solution)/shard_map/psum | solution.py:231
  2086.5 245.9 %all-reduce.9.cloned.1.call-done = (bf16[3,512,1024]{1,2,0:T(8,128)(2,1)}, bf16[1024,512]{1,0:T(8,128)(2,1)}, bf16[512,4096]{1,0:T(8,128)(2,1)}, bf16[4096,512]{1,0:T(8,128)(2,1)}) async-done(((bf16[3,512,1024]{1,2,0:T(8,128)(2,1)}, bf16[1024,512]{1,0:T(8,128)(2,1)}, bf16[512,4096]{1,0:T(8,128)(2,1)}, bf16[4096,512]{1,0:T(8,128)(2,1)}), (bf16[3,512,1024]{1,2,0:T(8,128)(2,1)}, bf16[1024,512]{1,0:T(8,128)(2,1)}, ...) | async-done | bytes 12582928 | tf_op jit(solution)/shard_map/psum | solution.py:258
  (263 shorter events, 161.5 us)
Async XLA Ops:
  7.2 223.3 %all-gather.8.cloned.1.call-start = ((), (), s32[]{:S(2)}) async-start(), calls=%async_computation.5 | async-start | bytes 15728640 | tf_op jit(solution)/shard_map/all_gather | solution.py:64
  8.0 303.2 %all-gather.12.cloned.1.call-start = ((), (), s32[]{:S(2)}) async-start(), calls=%async_computation.7 | async-start | bytes 5242880 | tf_op jit(solution)/shard_map/all_gather | solution.py:65
  8.7 349.1 %all-gather.10.cloned.1.call-start = ((), (), s32[]{:S(2)}) async-start(), calls=%async_computation.6 | async-start | bytes 2621440 | tf_op jit(solution)/shard_map/all_gather | solution.py:89
  8.8 221.8 %copy-start.14 = (f32[2048]{0:T(1024)}, f32[2048]{0:T(1024)S(1)}, u32[]{:S(2)}) copy-start(f32[2048]{0:T(1024)S(1)} %convert_element_type.155) | copy-start | bytes 24580
  8.8 221.8 %copy-start.30 = (f32[2048]{0:T(1024)}, f32[2048]{0:T(1024)S(1)}, u32[]{:S(2)}) copy-start(f32[2048]{0:T(1024)S(1)} %convert_element_type.156) | copy-start | bytes 24580
  9.4 221.2 %copy-start.16 = (f32[256]{0:T(256)}, f32[256]{0:T(256)S(1)}, u32[]{:S(2)}) copy-start(f32[256]{0:T(256)S(1)} %broadcast_multiply_fusion) | copy-start | bytes 3076
  9.8 220.8 %copy-start.26 = (f32[256]{0:T(256)}, f32[256]{0:T(256)S(1)}, u32[]{:S(2)}) copy-start(f32[256]{0:T(256)S(1)} %fusion.71) | copy-start | bytes 3076
  9.9 220.7 %copy-start.20 = (f32[256]{0:T(256)}, f32[256]{0:T(256)S(1)}, u32[]{:S(2)}) copy-start(f32[256]{0:T(256)S(1)} %fusion.94) | copy-start | bytes 3076
  244.9 159.6 %all-gather.18.cloned.1.call-start = ((), (), s32[]{:S(2)}) async-start(), calls=%async_computation.15 | async-start | bytes 2621440 | tf_op jit(solution)/shard_map/all_gather | solution.py:90
  247.1 64.0 %copy-start.6 = (bf16[1,256,2048]{2,1,0:T(8,128)(2,1)S(1)}, bf16[1,256,2048]{2,1,0:T(8,128)(2,1)}, u32[]{:S(2)}) copy-start(bf16[1,256,2048]{2,1,0:T(8,128)(2,1)} %param.35) | copy-start | bytes 3145732
  247.1 444.3 %all-gather.14.cloned.1.call-start = ((), (), s32[]{:S(2)}) async-start(), calls=%async_computation.8 | async-start | bytes 20971520 | tf_op jit(solution)/shard_map/all_gather | solution.py:66
  247.7 730.1 %all-gather.16.cloned.1.call-start = ((), (), s32[]{:S(2)}) async-start(), calls=%async_computation.9 | async-start | bytes 20971520 | tf_op jit(solution)/shard_map/all_gather | solution.py:67
  248.3 807.4 %reduce-scatter.6.cloned.1.call-start = ((), (), s32[]{:S(2)}) async-start(), calls=%async_computation.10 | async-start | bytes 5242880 | tf_op jit(solution)/shard_map/reduce_scatter | solution.py:202
  469.5 221.9 %copy-start.1 = (bf16[1,256,2048]{2,1,0:T(8,128)(2,1)S(1)}, bf16[1,256,2048]{2,1,0:T(8,128)(2,1)}, u32[]{:S(2)}) copy-start(bf16[1,256,2048]{2,1,0:T(8,128)(2,1)} %param.21) | copy-start | bytes 3145732
  469.5 221.9 %copy-start.17 = (f32[256]{0:T(256)S(1)}, f32[256]{0:T(256)}, u32[]{:S(2)}) copy-start(f32[256]{0:T(256)} %copy-done.16) | copy-start | bytes 3076
  469.5 221.9 %copy-start.21 = (f32[256]{0:T(256)S(1)}, f32[256]{0:T(256)}, u32[]{:S(2)}) copy-start(f32[256]{0:T(256)} %copy-done.20) | copy-start | bytes 3076
  469.5 221.9 %copy-start.23 = (f32[4096]{0:T(1024)S(1)}, f32[4096]{0:T(1024)}, u32[]{:S(2)}) copy-start(f32[4096]{0:T(1024)} %convert_element_type.167) | copy-start | bytes 49156
  470.9 649.1 %all-reduce.11.cloned.1.call-start = ((), (), s32[]{:S(2)}) async-start(), calls=%async_computation.18 | async-start | bytes 6291456 | tf_op jit(solution)/shard_map/psum | solution.py:151
  1083.8 104.8 %reduce-scatter.10.cloned.1.call-start = ((), (), s32[]{:S(2)}) async-start(), calls=%async_computation.12 | async-start | bytes 5242880 | tf_op jit(solution)/shard_map/reduce_scatter | solution.py:247
  1087.1 316.2 %reduce-scatter.8.cloned.1.call-start = ((), (), s32[]{:S(2)}) async-start(), calls=%async_computation.11 | async-start | bytes 15728640 | tf_op jit(solution)/shard_map/reduce_scatter | solution.py:244
  1096.2 591.0 %reduce-scatter.12.cloned.1.call-start = ((), (), s32[]{:S(2)}) async-start(), calls=%async_computation.13 | async-start | bytes 20971520 | tf_op jit(solution)/shard_map/reduce_scatter | solution.py:250
  1107.3 863.1 %reduce-scatter.14.cloned.1.call-start = ((), (), s32[]{:S(2)}) async-start(), calls=%async_computation.14 | async-start | bytes 20971520 | tf_op jit(solution)/shard_map/reduce_scatter | solution.py:253
  1117.2 969.4 %all-reduce.7.cloned.1.call-start = ((), (), s32[]{:S(2)}) async-start(), calls=%async_computation.16 | async-start | bytes 147456 | tf_op jit(solution)/shard_map/psum | solution.py:231
  1131.7 1200.8 %all-reduce.9.cloned.1.call-start = ((), (), s32[]{:S(2)}) async-start(), calls=%async_computation.17 | async-start | bytes 25165824 | tf_op jit(solution)/shard_map/psum | solution.py:258
  (37 other events, 155.1 us)
Sparse Core Ops, SparseCore 0:
  9.6 220.8 all-gather.7
  232.1 78.9 all-gather.11
  313.3 44.4 all-gather.9
  359.8 44.6 all-gather.17
  405.9 285.4 all-gather.13
  692.8 284.9 all-gather.15
  980.7 74.9 reduce-scatter.5
  1083.9 23.8 all-reduce.10
  1110.6 77.9 reduce-scatter.9
  1190.9 212.3 reduce-scatter.7
  1405.8 281.3 reduce-scatter.11
  1689.4 281.0 reduce-scatter.13
  1979.1 107.3 all-reduce.6
  2090.8 241.6 all-reduce.8
where the time goes:
time: 2370 us; the launch traced here: 2360 us
  waiting for transfers between devices  2090 us (88%)
  matrix products  142 us (6%)
  local copies, waits for them, and re-layouts  63.1 us (3%)
  other arithmetic  49.8 us (2%)
    reduce_scatter x1, waiting for transfers between devices, per_device(): lax.psum_scatter(up_grad.astype(jnp.bfloat16), 'ctx', scatter_dimension=0...  284 us
    reduce_scatter x1, waiting for transfers between devices, per_device(): lax.psum_scatter(down_grad.astype(jnp.bfloat16), 'ctx', scatter_dimension...  283 us
    all_gather x1, waiting for transfers between devices, per_device(): lax.all_gather(down_weight, 'ctx', axis=1, tiled=True)  268 us
    psum x1, waiting for transfers between devices, per_device(): lax.psum(slices[0].astype(jnp.bfloat16), 'stream').astype(jnp.float32)  246 us
    all_gather x1, waiting for transfers between devices, per_device(): lax.all_gather(up_weight, 'ctx', axis=0, tiled=True)  220 us
    all_gather x1, waiting for transfers between devices, per_device(): lax.all_gather(qkv_weight, 'ctx', axis=1, tiled=True)  220 us
    reduce_scatter x1, waiting for transfers between devices, per_device(): lax.psum_scatter(qkv_grad.astype(jnp.bfloat16), 'ctx', scatter_dimension=...  215 us
    psum x1, waiting for transfers between devices, per_device(): lax.psum((gain_grad_one, offset_grad_one, qkv_bias_grad, bias_grad, gain_...  116 us
  transfers between devices with their start and end apart: 14, of which 13 were waited for; matrix products, arithmetic and copies ran while one was open for 8% of the time, Pallas kernels for 0%

commit v1 on v0

--- a/solution.py
+++ b/solution.py
@@ -255,7 +255,9 @@
         ).astype(jnp.float32),
     )
     shards = (
-        lax.psum(slices[0].astype(jnp.bfloat16), "stream").astype(jnp.float32),
+        jnp.sum(lax.all_gather(slices[0].astype(jnp.bfloat16), "stream"), axis=0).astype(
+            jnp.float32
+        ),
         lax.psum(slices[1].astype(jnp.bfloat16), "stream").astype(jnp.float32),
         lax.psum(slices[2].astype(jnp.bfloat16), "stream").astype(jnp.float32),
         lax.psum(slices[3].astype(jnp.bfloat16), "stream").astype(jnp.float32),

time: 2370 us -> 2440 us (1.030)
  waiting for transfers between devices: 2090 us -> 2140 us
    all_gather x0 -> x1, waiting for transfers between devices: none -> 110 us  [per_device(): lax.all_gather(slices[0].astype(jnp.bfloat16), 'stream')]
    psum x1, waiting for transfers between devices: 246 us -> 194 us  [per_device(): lax.psum(slices[1].astype(jnp.bfloat16), 'stream').astype(jnp.float32)]
  transfers between devices with their start and end apart: 14 -> 15, of which waited for: 13 -> 14; matrix products, arithmetic and copies ran while one was open for 8% -> 9% of each run, Pallas kernels for 0% -> 0%
where the time goes in v1:
time: 2440 us; the launch traced here: 2430 us
  waiting for transfers between devices  2140 us (88%)
  matrix products  142 us (6%)
  local copies, waits for them, and re-layouts  72.8 us (3%)
  other arithmetic  59.6 us (2%)
    reduce_scatter x1, waiting for transfers between devices, per_device(): lax.psum_scatter(down_grad.astype(jnp.bfloat16), 'ctx', scatter_dimension...  283 us
    reduce_scatter x1, waiting for transfers between devices, per_device(): lax.psum_scatter(up_grad.astype(jnp.bfloat16), 'ctx', scatter_dimension=0...  283 us
    all_gather x1, waiting for transfers between devices, per_device(): lax.all_gather(down_weight, 'ctx', axis=1, tiled=True)  268 us
    all_gather x1, waiting for transfers between devices, per_device(): lax.all_gather(qkv_weight, 'ctx', axis=1, tiled=True)  220 us
    all_gather x1, waiting for transfers between devices, per_device(): lax.all_gather(up_weight, 'ctx', axis=0, tiled=True)  220 us
    reduce_scatter x1, waiting for transfers between devices, per_device(): lax.psum_scatter(qkv_grad.astype(jnp.bfloat16), 'ctx', scatter_dimension=...  215 us
    psum x1, waiting for transfers between devices, per_device(): lax.psum(slices[1].astype(jnp.bfloat16), 'stream').astype(jnp.float32)  194 us
    psum x1, waiting for transfers between devices, per_device(): lax.psum((gain_grad_one, offset_grad_one, qkv_bias_grad, bias_grad, gain_...  111 us
  transfers between devices with their start and end apart: 15, of which 14 were waited for; matrix products, arithmetic and copies ran while one was open for 9% of the time, Pallas kernels for 0%

profile of v1, /device:TPU:0, one launch (start us, length us, event | category | flops | bytes accessed | tf_op | source)
XLA Modules:
  0.0 2434.5 jit_solution(8636821777642325991)
XLA Ops:
  10.8 219.8 %all-gather.10.cloned.1.call-done = bf16[3,2048,1024]{2,1,0:T(8,128)(2,1)} async-done(((bf16[3,512,1024]{2,1,0:T(8,128)(2,1)}), bf16[3,2048,1024]{2,1,0:T(8,128)(2,1)}) %all-gather.10.cloned.1.call-update) | async-done | bytes 12582928 | tf_op jit(solution)/shard_map/all_gather | solution.py:64
  249.3 61.9 %all-gather.14.cloned.1.call-done = bf16[1024,2048]{1,0:T(8,128)(2,1)} async-done(((bf16[1024,512]{1,0:T(8,128)(2,1)}), bf16[1024,2048]{1,0:T(8,128)(2,1)}) %all-gather.14.cloned.1.call-update) | async-done | bytes 4194320 | tf_op jit(solution)/shard_map/all_gather | solution.py:65
  315.9 41.9 %all-gather.12.cloned.1.call-done = bf16[1024,1024]{1,0:T(8,128)(2,1)} async-done(((bf16[256,1024]{1,0:T(8,128)(2,1)}), bf16[1024,1024]{1,0:T(8,128)(2,1)}) %all-gather.12.cloned.1.call-update) | async-done | bytes 2097168 | tf_op jit(solution)/shard_map/all_gather | solution.py:89
  362.7 41.8 %all-gather.20.cloned.1.call-done = bf16[1,1024,1024]{2,1,0:T(8,128)(2,1)} async-done(((bf16[1,256,1024]{2,1,0:T(8,128)(2,1)}), bf16[1,1024,1024]{2,1,0:T(8,128)(2,1)}) %all-gather.20.cloned.1.call-update) | async-done | bytes 2097168 | tf_op jit(solution)/shard_map/all_gather | solution.py:90
  417.1 14.8 while.38
  434.6 29.0 %while.39 = (s32[]{:T(128)}, f32[256,4,256]{0,2,1:T(8,128)}, bf16[2,512,2048]{1,2,0:T(8,128)(2,1)}, bf16[2,512,4,256]{3,1,2,0:T(8,128)(2,1)}, s32[2]{0:T(128)S(1...) while((s32[]{:T(128)}, f32[256,4,256]{0,2,1:T(8,128)}, ...), condition=%wide.region_13.14_spmd.clone, body=%wide.region_12.13_spmd.clone.sunk | while | flops 1352794880 | bytes 31735028 | solution.py:197
  471.7 219.8 %all-gather.16.cloned.1.call-done = bf16[2048,4096]{1,0:T(8,128)(2,1)} async-done(((bf16[512,4096]{1,0:T(8,128)(2,1)}), bf16[2048,4096]{1,0:T(8,128)(2,1)}) %all-gather.16.cloned.1.call-update) | async-done | bytes 16777232 | tf_op jit(solution)/shard_map/all_gather | solution.py:66
  691.4 18.6 multiply_convert_fusion
  710.0 267.8 %all-gather.18.cloned.1.call-done = bf16[4096,2048]{1,0:T(8,128)(2,1)} async-done(((bf16[4096,512]{1,0:T(8,128)(2,1)}), bf16[4096,2048]{1,0:T(8,128)(2,1)}) %all-gather.18.cloned.1.call-update) | async-done | bytes 16777232 | tf_op jit(solution)/shard_map/all_gather | solution.py:67
  977.9 8.9 fusion.102
  989.6 19.1 convert_reduce_fusion
  1008.7 12.0 convolution_convert_fusion.3
  1020.7 35.0 %reduce-scatter.6.cloned.1.call-done = bf16[256,2048]{1,0:T(8,128)(2,1)} async-done(((bf16[1024,2048]{1,0:T(8,128)(2,1)}), bf16[256,2048]{1,0:T(8,128)(2,1)}) %reduce-scatter.6.cloned.1.call-update) | async-done | bytes 1048592 | tf_op jit(solution)/shard_map/reduce_scatter | solution.py:202
  1074.4 9.3 fusion.64
  1087.2 10.3 convolution_convert_fusion.1
  1097.6 10.8 convolution_convert_fusion
  1131.8 56.8 %reduce-scatter.10.cloned.1.call-done = bf16[1024,512]{1,0:T(8,128)(2,1)} async-done(((bf16[1024,2048]{1,0:T(8,128)(2,1)}), bf16[1024,512]{1,0:T(8,128)(2,1)}) %reduce-scatter.10.cloned.1.call-update) | async-done | bytes 1048592 | tf_op jit(solution)/shard_map/reduce_scatter | solution.py:247
  1188.6 283.2 %reduce-scatter.12.cloned.1.call-done = bf16[512,4096]{1,0:T(8,128)(2,1)} async-done(((bf16[2048,4096]{1,0:T(8,128)(2,1)}), bf16[512,4096]{1,0:T(8,128)(2,1)}) %reduce-scatter.12.cloned.1.call-update) | async-done | bytes 4194320 | tf_op jit(solution)/shard_map/reduce_scatter | solution.py:250
  1471.8 283.4 %reduce-scatter.14.cloned.1.call-done = bf16[4096,512]{1,0:T(8,128)(2,1)} async-done(((bf16[4096,2048]{1,0:T(8,128)(2,1)}), bf16[4096,512]{1,0:T(8,128)(2,1)}) %reduce-scatter.14.cloned.1.call-update) | async-done | bytes 4194320 | tf_op jit(solution)/shard_map/reduce_scatter | solution.py:253
  1755.3 214.9 %reduce-scatter.8.cloned.1.call-done = bf16[3,512,1024]{1,2,0:T(8,128)(2,1)} async-done(((bf16[3,2048,1024]{1,2,0:T(8,128)(2,1)}), bf16[3,512,1024]{1,2,0:T(8,128)(2,1)}) %reduce-scatter.8.cloned.1.call-update) | async-done | bytes 3145744 | tf_op jit(solution)/shard_map/reduce_scatter | solution.py:244
  1975.0 111.5 %all-reduce.7.cloned.1.call-done = (f32[2048]{0:T(1024)}, f32[2048]{0:T(1024)}, f32[3,1024]{1,0:T(4,128)}, f32[2048]{0:T(1024)}, f32[2048]{0:T(1024)}, /*index=5*/f32[2048]{0:T(1024)}, f32[4096]{0:T(1024)}) async-done(((f32[2048]{0:T(1024)}, f32[2048]{0:T(1024)}, f32[3,1024]{1,0:T(4,128)}, f32[2048]{0:T(1024)}, f32[2048]{0:T(1024)}, /*index=5*/f32[2048]{0:T(1024)}, f32[4096]{0:T(1024)}), (f32[2048]{0:T(1024)}, ...) | async-done | bytes 69648 | tf_op jit(solution)/shard_map/psum | solution.py:231
  2086.5 194.0 %all-reduce.9.cloned.1.call-done = (bf16[1024,512]{1,0:T(8,128)(2,1)}, bf16[512,4096]{1,0:T(8,128)(2,1)}, bf16[4096,512]{1,0:T(8,128)(2,1)}) async-done(((bf16[1024,512]{1,0:T(8,128)(2,1)}, bf16[512,4096]{1,0:T(8,128)(2,1)}, bf16[4096,512]{1,0:T(8,128)(2,1)}), (bf16[1024,512]{1,0:T(8,128)(2,1)}, bf16[512,4096]{1,0:T(8,128)(2,1)}, bf16[4096,512]{1,0:T(8,128)(2,1)})) %all-reduce.9.cloned.1.call-update) | async-done | bytes 9437200 | tf_op jit(solution)/shard_map/psum | solution.py:261
  2295.9 109.6 %all-gather.22.cloned.1.call-done = bf16[12,512,1024]{2,1,0:T(8,128)(2,1)} async-done(((bf16[3,512,1024]{2,1,0:T(8,128)(2,1)}), bf16[12,512,1024]{2,1,0:T(8,128)(2,1)}) %all-gather.22.cloned.1.call-update) | async-done | bytes 12582928 | tf_op jit(solution)/shard_map/all_gather | solution.py:258
  2405.5 8.7 reduce_sum.162
  (267 shorter events, 188.4 us)
Async XLA Ops:
  7.2 223.3 %all-gather.10.cloned.1.call-start = ((), (), s32[]{:S(2)}) async-start(), calls=%async_computation.5 | async-start | bytes 15728640 | tf_op jit(solution)/shard_map/all_gather | solution.py:64
  8.0 303.2 %all-gather.14.cloned.1.call-start = ((), (), s32[]{:S(2)}) async-start(), calls=%async_computation.7 | async-start | bytes 5242880 | tf_op jit(solution)/shard_map/all_gather | solution.py:65
  8.7 349.1 %all-gather.12.cloned.1.call-start = ((), (), s32[]{:S(2)}) async-start(), calls=%async_computation.6 | async-start | bytes 2621440 | tf_op jit(solution)/shard_map/all_gather | solution.py:89
  8.8 221.8 %copy-start.13 = (f32[2048]{0:T(1024)}, f32[2048]{0:T(1024)S(1)}, u32[]{:S(2)}) copy-start(f32[2048]{0:T(1024)S(1)} %convert_element_type.157) | copy-start | bytes 24580
  8.8 221.8 %copy-start.29 = (f32[2048]{0:T(1024)}, f32[2048]{0:T(1024)S(1)}, u32[]{:S(2)}) copy-start(f32[2048]{0:T(1024)S(1)} %convert_element_type.158) | copy-start | bytes 24580
  9.4 221.2 %copy-start.15 = (f32[256]{0:T(256)}, f32[256]{0:T(256)S(1)}, u32[]{:S(2)}) copy-start(f32[256]{0:T(256)S(1)} %broadcast_multiply_fusion) | copy-start | bytes 3076
  9.8 220.8 %copy-start.25 = (f32[256]{0:T(256)}, f32[256]{0:T(256)S(1)}, u32[]{:S(2)}) copy-start(f32[256]{0:T(256)S(1)} %fusion.71) | copy-start | bytes 3076
  9.9 220.7 %copy-start.19 = (f32[256]{0:T(256)}, f32[256]{0:T(256)S(1)}, u32[]{:S(2)}) copy-start(f32[256]{0:T(256)S(1)} %fusion.94) | copy-start | bytes 3076
  244.9 159.6 %all-gather.20.cloned.1.call-start = ((), (), s32[]{:S(2)}) async-start(), calls=%async_computation.15 | async-start | bytes 2621440 | tf_op jit(solution)/shard_map/all_gather | solution.py:90
  247.1 444.3 %all-gather.16.cloned.1.call-start = ((), (), s32[]{:S(2)}) async-start(), calls=%async_computation.8 | async-start | bytes 20971520 | tf_op jit(solution)/shard_map/all_gather | solution.py:66
  247.7 730.1 %all-gather.18.cloned.1.call-start = ((), (), s32[]{:S(2)}) async-start(), calls=%async_computation.9 | async-start | bytes 20971520 | tf_op jit(solution)/shard_map/all_gather | solution.py:67
  248.3 807.4 %reduce-scatter.6.cloned.1.call-start = ((), (), s32[]{:S(2)}) async-start(), calls=%async_computation.10 | async-start | bytes 5242880 | tf_op jit(solution)/shard_map/reduce_scatter | solution.py:202
  469.8 221.6 %copy-start.1 = (bf16[1,256,2048]{2,1,0:T(8,128)(2,1)S(1)}, bf16[1,256,2048]{2,1,0:T(8,128)(2,1)}, u32[]{:S(2)}) copy-start(bf16[1,256,2048]{2,1,0:T(8,128)(2,1)} %param.21) | copy-start | bytes 3145732
  469.8 221.6 %copy-start.16 = (f32[256]{0:T(256)S(1)}, f32[256]{0:T(256)}, u32[]{:S(2)}) copy-start(f32[256]{0:T(256)} %copy-done.15) | copy-start | bytes 3076
  469.8 221.6 %copy-start.20 = (f32[256]{0:T(256)S(1)}, f32[256]{0:T(256)}, u32[]{:S(2)}) copy-start(f32[256]{0:T(256)} %copy-done.19) | copy-start | bytes 3076
  469.8 221.6 %copy-start.22 = (f32[4096]{0:T(1024)S(1)}, f32[4096]{0:T(1024)}, u32[]{:S(2)}) copy-start(f32[4096]{0:T(1024)} %convert_element_type.169) | copy-start | bytes 49156
  471.1 648.8 %all-reduce.11.cloned.1.call-start = ((), (), s32[]{:S(2)}) async-start(), calls=%async_computation.19 | async-start | bytes 6291456 | tf_op jit(solution)/shard_map/psum | solution.py:151
  1083.8 104.8 %reduce-scatter.10.cloned.1.call-start = ((), (), s32[]{:S(2)}) async-start(), calls=%async_computation.12 | async-start | bytes 5242880 | tf_op jit(solution)/shard_map/reduce_scatter | solution.py:247
  1087.1 384.7 %reduce-scatter.12.cloned.1.call-start = ((), (), s32[]{:S(2)}) async-start(), calls=%async_computation.13 | async-start | bytes 20971520 | tf_op jit(solution)/shard_map/reduce_scatter | solution.py:250
  1097.5 657.7 %reduce-scatter.14.cloned.1.call-start = ((), (), s32[]{:S(2)}) async-start(), calls=%async_computation.14 | async-start | bytes 20971520 | tf_op jit(solution)/shard_map/reduce_scatter | solution.py:253
  1108.4 861.8 %reduce-scatter.8.cloned.1.call-start = ((), (), s32[]{:S(2)}) async-start(), calls=%async_computation.11 | async-start | bytes 15728640 | tf_op jit(solution)/shard_map/reduce_scatter | solution.py:244
  1117.2 969.3 %all-reduce.7.cloned.1.call-start = ((), (), s32[]{:S(2)}) async-start(), calls=%async_computation.17 | async-start | bytes 147456 | tf_op jit(solution)/shard_map/psum | solution.py:231
  1131.7 1148.8 %all-reduce.9.cloned.1.call-start = ((), (), s32[]{:S(2)}) async-start(), calls=%async_computation.18 | async-start | bytes 18874368 | tf_op jit(solution)/shard_map/psum | solution.py:261
  1755.2 650.3 %all-gather.22.cloned.1.call-start = ((), (), s32[]{:S(2)}) async-start(), calls=%async_computation.16 | async-start | bytes 15728640 | tf_op jit(solution)/shard_map/all_gather | solution.py:258
  (37 other events, 217.6 us)
Sparse Core Ops, SparseCore 0:
  9.6 220.8 all-gather.9
  232.1 78.9 all-gather.13
  313.3 44.4 all-gather.11
  359.8 44.6 all-gather.19
  405.9 285.4 all-gather.15
  692.8 284.9 all-gather.17
  980.7 74.9 reduce-scatter.5
  1083.9 23.8 all-reduce.10
  1110.7 77.9 reduce-scatter.9
  1190.9 280.7 reduce-scatter.11
  1474.1 281.0 reduce-scatter.13
  1757.5 212.5 reduce-scatter.7
  1978.9 107.6 all-reduce.6
  2090.8 189.7 all-reduce.8
  2283.0 122.5 all-gather.21
